TPU v7x, 512 devices: a whole 4x4x16 slice. The times are simulated.
512 devices in a mesh: seg: 32 (over z, core), fsdp: 16 (over y, x).
Axes of the slice: x: 4, y: 4, z: 16, core: 2. Of those that a mesh axis runs over, the one named last changes fastest.
Arguments:
- frames: bfloat16 [16, 256, 16, 1024], P('fsdp', 'seg'), may hold values from -6 to 6
- memory_in: bfloat16 [16, 256, 1024], P('fsdp', 'seg'), may hold values from -6 to 6
- lengths: int32 [16], P('fsdp'), may hold values from 1 to 256, as said below
- ln_gain: float32 [1024], replicated, may hold values from 0.25 to 1.75
- w_query: bfloat16 [1024, 1024], P('fsdp'), may hold values from -1 to 1
- w_key: bfloat16 [1024, 1024], P('fsdp'), may hold values from -12 to 12
- w_value: bfloat16 [1024, 1024], P('fsdp'), may hold values from -0.1875 to 0.1875
- w_out: bfloat16 [1024, 1024], P('fsdp'), may hold values from -0.1875 to 0.1875
- grad_frames: bfloat16 [16, 256, 16, 1024], P('fsdp', 'seg'), may hold values from -6 to 6
- grad_memory: bfloat16 [16, 256, 1024], P('fsdp', 'seg'), may hold values from -6 to 6
Outputs:
- frames_out: bfloat16 [16, 256, 16, 1024], P('fsdp', 'seg')
- memory_out: bfloat16 [16, 256, 1024], P('fsdp', 'seg')
- value_grad: float32 [1024, 1024], P('fsdp')
Inputs may be any that keep to these rules, and one draw needn't show every extreme that they name: `lengths`: in every aligned block of 1 utterances (those of one fsdp index) at least one has length 256.
All inputs are finite; a program needn't handle non-finite values.
Results may differ from a plain program's by a relative error of at most 0.04.
Values may be sent and summed in bfloat16 or wider, within the bound.
A program may use at most 64 MiB of HBM per device.

v0:
```python
import math

import jax
import jax.numpy as jnp
from jax import lax
from jax.sharding import PartitionSpec as P

HEADS = 16
LEFT = 16
MEMORY = 8


epsilon = 1e-05
masked_score = -1e30


def passed_along(array, axis, by):
    size = lax.axis_size(axis)
    pairs = [(i, i + by) for i in range(size) if 0 <= i + by < size]
    return lax.ppermute(array, axis, pairs)


def on_device(
    frames, memory_in, lengths, ln_gain, w_query, w_key, w_value, w_out, grad_frames, grad_memory
):
    utterances = frames.shape[0]
    local_segs = frames.shape[1]
    frame_count = frames.shape[2]
    model_width = frames.shape[3]
    head_dim = model_width // HEADS
    query_count = frame_count + 1
    segment = lax.axis_index("seg")
    first_global = segment * local_segs
    wide_frames = frames.astype(jnp.float32)
    row_mean = jnp.mean(wide_frames, axis=-1, keepdims=True)
    centred = wide_frames - row_mean
    row_var = jnp.mean(centred * centred, axis=-1, keepdims=True)
    normed = (centred * lax.rsqrt(row_var + epsilon) * ln_gain).astype(jnp.bfloat16)
    summary = jnp.mean(normed.astype(jnp.float32), axis=2).astype(jnp.bfloat16)
    query_rows = jnp.concatenate([normed, summary[:, :, None, :]], axis=2)
    tail_rows = normed[:, local_segs - 1, frame_count - LEFT :]
    incoming = passed_along(tail_rows, "seg", 1)
    left_rows = jnp.concatenate(
        [incoming[:, None], normed[:, : local_segs - 1, frame_count - LEFT :]], axis=1
    )
    earlier = passed_along(memory_in, "seg", 1)
    extended = jnp.concatenate([earlier, memory_in], axis=1)
    local_pos = jnp.arange(local_segs)[:, None]
    slot_pos = jnp.arange(MEMORY)[None, :]
    bank_index = MEMORY + local_pos - 1 - slot_pos
    bank_valid = first_global + local_pos - 1 - slot_pos >= 0
    taken = jnp.take(extended, bank_index.reshape(-1), axis=1).reshape(
        utterances, local_segs, MEMORY, model_width
    )
    memory_rows = jnp.where(bank_valid[None, :, :, None], taken, jnp.zeros((), taken.dtype))
    key_rows = jnp.concatenate([memory_rows, left_rows, normed], axis=2)
    key_count = key_rows.shape[2]
    query_flat = query_rows.reshape(-1, model_width)
    key_flat = key_rows.reshape(-1, model_width)
    columns = query_flat
    queries = jnp.dot(
        columns,
        lax.all_gather(w_query, "fsdp", axis=0, tiled=True),
        preferred_element_type=jnp.float32,
    ).astype(jnp.bfloat16)
    columns = key_flat
    key_proj = jnp.dot(
        columns,
        lax.all_gather(w_key, "fsdp", axis=0, tiled=True),
        preferred_element_type=jnp.float32,
    )
    value_proj = jnp.dot(
        columns,
        lax.all_gather(w_value, "fsdp", axis=0, tiled=True),
        preferred_element_type=jnp.float32,
    )
    key_proj = key_proj.astype(jnp.bfloat16).reshape(
        utterances, local_segs, key_count, HEADS, head_dim
    )
    value_proj = value_proj.astype(jnp.bfloat16).reshape(
        utterances, local_segs, key_count, HEADS, head_dim
    )
    queries = queries.reshape(utterances, local_segs, query_count, HEADS, head_dim)
    scores = jnp.einsum(
        "utqhd,utkhd->uthqk", queries, key_proj, preferred_element_type=jnp.float32
    ) / math.sqrt(head_dim)
    key_slot = jnp.arange(key_count)[None, :]
    global_seg = first_global + local_pos
    valid_key = jnp.where(
        key_slot < MEMORY,
        global_seg - 1 - key_slot >= 0,
        jnp.where(key_slot < MEMORY + LEFT, global_seg >= 1, True),
    )
    scores = jnp.where(valid_key[None, :, None, None, :], scores, masked_score)
    highest = jnp.max(scores, axis=-1, keepdims=True)
    exponent = jnp.exp(scores - highest)
    soft_weights = (exponent / jnp.sum(exponent, axis=-1, keepdims=True)).astype(jnp.bfloat16)
    attended = jnp.einsum(
        "uthqk,utkhd->utqhd", soft_weights, value_proj, preferred_element_type=jnp.float32
    )
    attended = attended.astype(jnp.bfloat16).reshape(-1, model_width)
    upstream = jnp.concatenate([grad_frames, grad_memory[:, :, None, :]], axis=2).reshape(
        -1, model_width
    )
    columns = attended
    projected = jnp.dot(
        columns,
        lax.all_gather(w_out, "fsdp", axis=0, tiled=True),
        preferred_element_type=jnp.float32,
    )
    back_proj = lax.dot_general(
        upstream,
        lax.all_gather(w_out, "fsdp", axis=0, tiled=True),
        (((1,), (1,)), ((), ())),
        preferred_element_type=jnp.float32,
    )
    projected = projected.reshape(utterances, local_segs, query_count, model_width)
    live_mask = (first_global + jnp.arange(local_segs)[None, :] < lengths[:, None]).astype(
        jnp.float32
    )
    frames_out = (wide_frames + live_mask[:, :, None, None] * projected[:, :, :frame_count]).astype(
        jnp.bfloat16
    )
    memory_out = (live_mask[:, :, None] * projected[:, :, frame_count]).astype(jnp.bfloat16)
    back_proj = back_proj.reshape(utterances, local_segs, query_count, model_width)
    grad_attended = (live_mask[:, :, None, None] * back_proj).astype(jnp.bfloat16)
    grad_attended = grad_attended.reshape(utterances, local_segs, query_count, HEADS, head_dim)
    grad_values = jnp.einsum(
        "uthqk,utqhd->utkhd", soft_weights, grad_attended, preferred_element_type=jnp.float32
    )
    grad_values = grad_values.astype(jnp.bfloat16).reshape(-1, model_width)
    columns = key_flat
    grad_part = lax.psum_scatter(
        lax.dot_general(
            columns, grad_values, (((0,), (0,)), ((), ())), preferred_element_type=jnp.float32
        ).astype(jnp.bfloat16),
        "fsdp",
        scatter_dimension=0,
        tiled=True,
    )
    value_grad = lax.psum(grad_part, "seg").astype(jnp.float32)
    return (frames_out, memory_out, value_grad)


def solution(mesh):
    return jax.shard_map(
        on_device,
        mesh=mesh,
        in_specs=(
            P("fsdp", "seg", None, None),
            P("fsdp", "seg", None),
            P("fsdp"),
            P(),
            P("fsdp", None),
            P("fsdp", None),
            P("fsdp", None),
            P("fsdp", None),
            P("fsdp", "seg", None, None),
            P("fsdp", "seg", None),
        ),
        out_specs=(P("fsdp", "seg", None, None), P("fsdp", "seg", None), P("fsdp", None)),
        check_vma=False,
    )
```

profile of v0, /device:TPU:1, one launch (start us, length us, event | category | flops | bytes accessed | tf_op | source)
XLA Modules:
  0.0 568.1 jit_solution(2089565964976708697)
XLA Ops:
  7.2 0.0 all-gather.9.cloned.1.call-start
  7.2 0.7 all-gather.9.cloned.1.call-update
  7.9 0.0 all-gather.7.cloned.1.call-start
  8.0 0.7 all-gather.7.cloned.1.call-update
  8.7 0.0 all-gather.11.cloned.1.call-start
  8.7 0.7 all-gather.11.cloned.1.call-update
  9.4 0.0 all-gather.5.cloned.1.call-start
  9.4 1.1 convert_reduce_fusion
  10.5 0.0 copy-start.7
  10.5 1.1 fusion.26
  11.7 1.3 convert_reduce_fusion.1
  13.0 4.9 collective-permute-start.1
  17.9 1.9 collective-permute-start
  19.8 0.0 all-gather.5.cloned.1.call-update
  19.9 0.0 reduce-scatter.2.cloned.1.call-start
  19.9 0.1 iota_subtract_fusion
  20.0 0.1 sub.104
  20.8 0.1 pad_maximum_fusion.1
  20.9 0.1 subtract_compare_fusion.1
  21.0 0.1 fusion.36
  21.1 0.1 reshape.360
  21.2 1.8 collective-permute-done
  23.1 0.7 gather_fusion
  23.8 0.1 fusion.32
  23.9 0.0 collective-permute-done.1
  23.9 0.1 pad_maximum_fusion
  24.0 51.0 %all-gather.9.cloned.1.call-done = bf16[1024,1024]{1,0:T(8,128)(2,1)} async-done(((bf16[64,1024]{1,0:T(8,128)(2,1)}), bf16[1024,1024]{1,0:T(8,128)(2,1)}) %all-gather.9.cloned.1.call-update) | async-done | bytes 2097168 | tf_op jit(solution)/shard_map/all_gather | solution.py:69
  75.0 2.4 convolution_convert_fusion.3
  77.4 0.8 reshape.362
  78.2 0.0 copy-start.9
  78.2 59.4 %all-gather.7.cloned.1.call-done = bf16[1024,1024]{1,0:T(8,128)(2,1)} async-done(((bf16[64,1024]{1,0:T(8,128)(2,1)}), bf16[1024,1024]{1,0:T(8,128)(2,1)}) %all-gather.7.cloned.1.call-update) | async-done | bytes 2097168 | tf_op jit(solution)/shard_map/all_gather | solution.py:63
  137.7 2.1 convolution_convert_fusion.5
  139.7 0.4 reshape.361
  140.1 60.3 %all-gather.11.cloned.1.call-done = bf16[1024,1024]{1,0:T(8,128)(2,1)} async-done(((bf16[64,1024]{1,0:T(8,128)(2,1)}), bf16[1024,1024]{1,0:T(8,128)(2,1)}) %all-gather.11.cloned.1.call-update) | async-done | bytes 2097168 | tf_op jit(solution)/shard_map/all_gather | solution.py:108
  200.4 2.4 fusion.19
  202.8 1.2 reshape.379
  204.0 0.8 multiply_select_fusion
  204.8 1.0 fusion.42
  205.8 0.0 copy-start.5
  205.8 0.6 copy-done.5
  206.4 6.9 %fusion.7 = bf16[1,8,40,16,64]{4,2,3,1,0:T(8,128)(2,1)} fusion(bf16[8,17,16,64]{3,2,1,0:T(8,128)(2,1)S(1)} %copy-done.4, f32[8,16,17]{2,1,0:T(8,128)S(1)} %fusion.42, f32[8,16,17,40]{3,2,1,0:T(8,128)S(1)} %multiply_select_fusion), kind=kOutput, calls=%fused_computation.12 | convolution fusion | flops 11732135 | bytes 1290752 | tf_op jit(solution)/shard_map/uthqk,utqhd->utkhd/dot_general | solution.py:128
  213.4 1.5 copy.27
  214.9 1.7 reshape.365
  216.6 3.7 convolution_convert_fusion
  220.3 0.0 reduce-scatter.2.cloned.1.call-update
  220.3 0.2 all-reduce.2.cloned.1.call-start
  220.6 42.4 %all-gather.5.cloned.1.call-done = bf16[1024,1024]{1,0:T(8,128)(2,1)} async-done(((bf16[64,1024]{1,0:T(8,128)(2,1)}), bf16[1024,1024]{1,0:T(8,128)(2,1)}) %all-gather.5.cloned.1.call-update) | async-done | bytes 2097168 | tf_op jit(solution)/shard_map/all_gather | solution.py:74
  262.9 3.3 convolution_convert_fusion.4
  266.2 2.0 reshape.359
  268.2 0.0 copy-done.6
  268.2 6.4 %fusion.10 = bf16[1,8,17,16,64]{4,2,3,1,0:T(8,128)(2,1)} fusion(bf16[8,40,16,64]{3,2,1,0:T(8,128)(2,1)S(1)} %reshape.359, f32[8,16,17]{2,1,0:T(8,128)S(1)} %copy-done.6, f32[8,16,17,40]{3,2,1,0:T(8,128)S(1)} %multiply_select_fusion), kind=kOutput, calls=%fused_computation.18 | convolution fusion | flops 11543719 | bytes 1290752 | tf_op jit(solution)/shard_map/uthqk,utkhd->utqhd/dot_general | solution.py:98
  274.6 1.4 copy.29
  275.9 0.5 reshape.378
  276.4 0.0 copy-done.1
  276.4 0.0 copy-start
  276.4 0.6 fusion.13
  277.0 0.3 copy-done
  277.4 0.8 fusion.29
  278.2 78.8 %reduce-scatter.2.cloned.1.call-done = bf16[64,1024]{1,0:T(8,128)(2,1)} async-done(((bf16[1024,1024]{1,0:T(8,128)(2,1)}), bf16[64,1024]{1,0:T(8,128)(2,1)}) %reduce-scatter.2.cloned.1.call-update) | async-done | bytes 131088 | tf_op jit(solution)/shard_map/reduce_scatter | solution.py:133
  357.0 0.0 all-reduce.2.cloned.1.call-update
  357.1 0.1 fusion.34
  357.1 0.6 copy.28
  357.8 201.9 %all-reduce.2.cloned.1.call-done = bf16[64,1024]{1,0:T(8,128)(2,1)} async-done(((bf16[64,1024]{1,0:T(8,128)(2,1)}), bf16[64,1024]{1,0:T(8,128)(2,1)}) %all-reduce.2.cloned.1.call-update) | async-done | bytes 131088 | tf_op jit(solution)/shard_map/psum | solution.py:141
  559.6 1.6 convert_element_type.112
  (27 shorter events, 0.2 us)
Async XLA Ops:
  7.2 10.7 %copy-start.8 = (bf16[1,8,1024]{2,1,0:T(8,128)(2,1)S(1)}, bf16[1,8,1024]{2,1,0:T(8,128)(2,1)}, u32[]{:S(2)}) copy-start(bf16[1,8,1024]{2,1,0:T(8,128)(2,1)} %param.11) | copy-start | bytes 49156
  7.2 67.8 %all-gather.9.cloned.1.call-start = ((), (), s32[]{:S(2)}) async-start(), calls=%async_computation.3 | async-start | bytes 2228224 | tf_op jit(solution)/shard_map/all_gather | solution.py:69
  7.9 129.8 %all-gather.7.cloned.1.call-start = ((), (), s32[]{:S(2)}) async-start(), calls=%async_computation.2 | async-start | bytes 2228224 | tf_op jit(solution)/shard_map/all_gather | solution.py:63
  8.7 191.7 %all-gather.11.cloned.1.call-start = ((), (), s32[]{:S(2)}) async-start(), calls=%async_computation.4 | async-start | bytes 2228224 | tf_op jit(solution)/shard_map/all_gather | solution.py:108
  9.4 253.6 %all-gather.5.cloned.1.call-start = ((), (), s32[]{:S(2)}) async-start(), calls=%async_computation.1 | async-start | bytes 2228224 | tf_op jit(solution)/shard_map/all_gather | solution.py:74
  10.5 10.7 %copy-start.7 = (bf16[1,8,1024]{2,1,0:T(8,128)(2,1)S(1)}, bf16[1,8,1024]{2,1,0:T(8,128)(2,1)}, u32[]{:S(2)}) copy-start(bf16[1,8,1024]{2,1,0:T(8,128)(2,1)} %param.19) | copy-start | bytes 49156
  13.0 10.9 %collective-permute-start.1 = (bf16[1,16,1024]{2,1,0:T(8,128)(2,1)S(1)}, bf16[1,16,1024]{2,1,0:T(8,128)(2,1)S(1)}, u32[]{:S(2)}, u32[]{:S(2)}) collective-permute-start(bf16[1,16,1024]{2,1,0:T(8,128)(2,1)S(1)} %slice_bitcast_fusion.1), channel_id=1, source_target_pairs={{0,16},{16,32},{32,48},{48,64},{64,80},{80,96},{96,112},{112,128},... | collective-permute-start | bytes 98312 | tf_op jit(solution)/shard_map/ppermute | solution.py:20
  17.9 5.2 collective-permute-start
  19.9 337.2 %reduce-scatter.2.cloned.1.call-start = ((), (), s32[]{:S(2)}) async-start(), calls=%async_computation.5 | async-start | bytes 2228224 | tf_op jit(solution)/shard_map/reduce_scatter | solution.py:133
  23.9 53.5 %copy-start.2 = (bf16[1,8,40,1024]{3,2,1,0:T(8,128)(2,1)}, bf16[1,8,40,1024]{3,2,1,0:T(8,128)(2,1)S(1)}, u32[]{:S(2)}) copy-start(bf16[1,8,40,1024]{3,2,1,0:T(8,128)(2,1)S(1)} %pad_maximum_fusion) | copy-start | bytes 1966084
  78.2 122.1 %copy-start.9 = (bf16[1,8,16,1024]{3,2,1,0:T(8,128)(2,1)S(1)}, bf16[1,8,16,1024]{3,2,1,0:T(8,128)(2,1)}, u32[]{:S(2)}) copy-start(bf16[1,8,16,1024]{3,2,1,0:T(8,128)(2,1)} %param.18) | copy-start | bytes 786436
  204.8 1.6 copy-start.4
  205.8 0.6 copy-start.5
  214.9 1.7 copy-start.3
  220.3 339.3 %all-reduce.2.cloned.1.call-start = ((), (), s32[]{:S(2)}) async-start(), calls=%async_computation.6 | async-start | bytes 262144 | tf_op jit(solution)/shard_map/psum | solution.py:141
  266.2 2.0 copy-start.6
  274.6 1.8 copy-start.1
  276.4 1.0 copy-start
Sparse Core Ops, SparseCore 0:
  11.0 63.9 all-gather.8
  78.0 59.6 all-gather.6
  140.7 59.6 all-gather.10
  203.2 59.6 all-gather.4
  266.9 90.0 reduce-scatter.1
  359.2 200.3 all-reduce.1
where the time goes:
time: 569 us; the launch traced here: 568 us
  waiting for transfers between devices  498 us (88%)
  matrix products  28.6 us (5%)
  between operations  15.1 us (3%)
  local copies, waits for them, and re-layouts  12 us (2%)
  other arithmetic  7.43 us (1%)
  starting transfers between devices  7.26 us (1%)
    psum x1, waiting for transfers between devices, on_device(): value_grad = lax.psum(grad_part, 'seg').astype(jnp.float32)  202 us
    reduce_scatter x1, waiting for transfers between devices, on_device(): lax.psum_scatter(lax.dot_general(columns, grad_values, (((0,), (0,)), (()...  78.8 us
    all_gather x1, waiting for transfers between devices, on_device(): lax.all_gather(w_out, 'fsdp', axis=0, tiled=True)  60.3 us
    all_gather x1, waiting for transfers between devices, on_device(): lax.all_gather(w_query, 'fsdp', axis=0, tiled=True)  59.4 us
    all_gather x1, waiting for transfers between devices, on_device(): lax.all_gather(w_key, 'fsdp', axis=0, tiled=True)  51 us
    all_gather x1, waiting for transfers between devices, on_device(): lax.all_gather(w_value, 'fsdp', axis=0, tiled=True)  42.4 us
  transfers between devices with their start and end apart: 8, of which 7 were waited for; matrix products, arithmetic and copies ran while one was open for 8% of the time, Pallas kernels for 0%

commit v1 on v0

v1 whole, which is shorter than its diff:
```python
import functools

import jax
import jax.numpy as jnp
from jax import lax
from jax.experimental import pallas as pl
from jax.experimental.pallas import tpu as pltpu
from jax.sharding import PartitionSpec as P

F32 = jnp.float32
BF16 = jnp.bfloat16
MESH = pl.DeviceIdType.MESH
EPSILON = 1e-05
MASKED = -1e30
KEY, QUERY, OUT, VALUE = 0, 1, 2, 3
N_REMOTE = 120
N_LOCAL = 16


def mm(a, b):
    return jnp.dot(a, b, preferred_element_type=F32)


def kernel(
    frames, memory, lengths, gain, w_query, w_key, w_value, w_out, grad_frames, grad_memory,
    frames_out, memory_out, value_grad,
    W, WO2, fin, gin, mem, gmem, E, U, L, X, XT, bias, K, Q, V, PT, GA, GV, ATT, PP, PPR,
    G, RA1, RA2A, RA2B, SA, RS, RF, RB1, RB2A, RB2B, SB, T, ZS, ZR, ZQ, OB,
    fo_v, mo_v, gain_v,
    send_sem, recv_sem, local_sem,
):
    seg = lax.axis_index("seg")
    fsdp = lax.axis_index("fsdp")
    core = lax.rem(seg, 2)
    z = lax.div(seg, 2)
    x = lax.rem(fsdp, 4)
    y = lax.div(fsdp, 4)
    other = 1 - core
    quad = lax.div(z, 4)
    place = lax.rem(z, 4)

    def wrap(a, by, n=4):
        return lax.rem(a + by + n, n)

    def device(dx=0, dy=0, dz=0, flip=False, quad_by=None):
        c = other if flip else core
        if quad_by is None:
            zz = wrap(z, dz, 16)
        else:
            zz = quad * 4 + wrap(place, quad_by)
        return (zz * 2 + c, wrap(y, dy) * 4 + wrap(x, dx))

    counter = [0]

    def remote(src, dst, to):
        i = counter[0]
        counter[0] += 1
        copy = pltpu.make_async_remote_copy(
            src_ref=src, dst_ref=dst, send_sem=send_sem.at[i], recv_sem=recv_sem.at[i],
            device_id=to, device_id_type=MESH,
        )
        copy.start()
        sent.append(copy)
        return copy

    sent = []
    lcounter = [0]

    def local(src, dst):
        i = lcounter[0]
        lcounter[0] += 1
        copy = pltpu.make_async_copy(src, dst, local_sem.at[i])
        copy.start()
        return copy

    weights = (w_key, w_query, w_out, w_value)
    own_columns = pl.ds(pl.multiple_of(core * 512, 512), 512)
    own = []
    for m in range(4):
        own.append([
            local(weights[m].at[pl.ds(32 * d, 32), own_columns], W.at[m, y, x, d])
            for d in range(2)
        ])
    in_frames = local(frames, fin)
    in_gain = local(gain, gain_v)
    in_mem = local(memory, mem)
    in_grad = local(grad_frames, gin)
    in_gmem = local(grad_memory, gmem)

    partners = [device(dx=1), device(dx=-1), device(dy=1), device(dy=-1), device(flip=True)]
    partners += [device(dz=1), device(dz=-1), device(dz=4), device(dz=-4)]
    for k in (1, 2, 3):
        partners += [device(quad_by=k), device(quad_by=k, flip=True)]
    barrier = pltpu.get_barrier_semaphore()
    for partner in partners:
        pl.semaphore_signal(barrier, inc=1, device_id=partner, device_id_type=MESH)
    pl.semaphore_wait(barrier, len(partners))

    def first_to(d, s):
        return device(dx=s) if d == 0 else device(dy=s)

    def second_to(d, s):
        return device(dy=s) if d == 0 else device(dx=s)

    def ring_one(m):
        return {(d, s): remote(W.at[m, y, x, d], W.at[m, y, x, d], first_to(d, s))
                for s in (1, -1) for d in (0, 1)}

    def relay_one(m, came):
        out = {}
        for s in (1, -1):
            for d in (0, 1):
                came[d, s].wait_recv()
                rows = pl.ds(0 if s == 1 else 16, 16)
                ref = (W.at[m, y, wrap(x, -s), 0, rows] if d == 0
                       else W.at[m, wrap(y, -s), x, 1, rows])
                out[d, s] = remote(ref, ref, first_to(d, s))
        return out

    def ring_two(m, came):
        out = {}
        for d in (0, 1):
            for s in (1, -1):
                came[d, s].wait_recv()
        for s in (1, -1):
            for d in (0, 1):
                ref = W.at[m, y, :, 0] if d == 0 else W.at[m, :, x, 1]
                out[d, s] = remote(ref, ref, second_to(d, s))
        return out

    def relay_two(m, came):
        out = {}
        for s in (1, -1):
            for d in (0, 1):
                came[d, s].wait_recv()
                half = pl.ds(0 if s == 1 else 2, 2)
                ref = (W.at[m, wrap(y, -s), half, 0] if d == 0
                       else W.at[m, half, wrap(x, -s), 1])
                out[d, s] = remote(ref, ref, second_to(d, s))
        return out

    def finish(came):
        for s in (1, -1):
            for d in (0, 1):
                came[d, s].wait_recv()

    def weight(m):
        return W[m].reshape(1024, 512)

    one, one_relayed, two, two_relayed = {}, {}, {}, {}
    for m in range(4):
        for copy in own[m]:
            copy.wait()
        one[m] = ring_one(m)

    in_frames.wait()
    in_gain.wait()
    in_mem.wait()
    sums = []
    for t in range(8):
        rows = fin[16 * t:16 * t + 16, :].astype(F32)
        centred = rows - jnp.mean(rows, axis=-1, keepdims=True)
        var = jnp.mean(centred * centred, axis=-1, keepdims=True)
        normed = (centred * lax.rsqrt(var + EPSILON) * gain_v[...]).astype(BF16)
        E[core, 16 * t:16 * t + 16, :] = normed
        sums.append(jnp.mean(normed.astype(F32), axis=0, keepdims=True))
    zeros8 = jnp.zeros((8, 1024), F32)
    E[core, 128:144, :] = jnp.concatenate(sums + [zeros8], axis=0).astype(BF16)
    E[core, 144:160, :] = jnp.concatenate([mem[...].astype(F32), zeros8], axis=0).astype(BF16)
    rows_over = remote(E.at[core], E.at[core], device(flip=True))

    for m in range(4):
        one_relayed[m] = relay_one(m, one[m])

    in_grad.wait()
    in_gmem.wait()
    for h in range(2):
        cols = slice(512 * h, 512 * h + 512)
        U[core, h, 0:128, :] = gin[:, cols]
        U[core, h, 128:144, :] = jnp.concatenate(
            [gmem[:, cols].astype(F32), zeros8[:, :512]], axis=0).astype(BF16)
    grads_over = remote(U.at[core], U.at[core], device(flip=True))

    two[0] = ring_two(0, one_relayed[0])
    two[1] = ring_two(1, one_relayed[1])
    rows_over.wait_recv()
    tail_over = remote(E.at[1, 112:128], L.at[0], device(dz=1))
    bank_over = remote(E.at[1, 144:160], L.at[1], device(dz=1))

    slot = lax.broadcasted_iota(jnp.int32, (160, 144), 0)
    column = lax.broadcasted_iota(jnp.int32, (160, 144), 1)
    query_at = jnp.where(column < 128, column // 16, column - 128)
    key_at = jnp.where(slot < 144, slot // 16 - 1, slot - 152)
    reach = jnp.where(slot < 144, 1, 8)
    newest = jnp.where(slot < 144, 0, 1)
    back = query_at - key_at
    for g in range(2):
        base = (2 * z + g) * 8
        valid = (back >= newest) & (back <= reach) & (key_at + base >= 0)
        bias[g] = jnp.where(valid, 0.0, MASKED).astype(F32)

    X[0, 16:144, :] = E[0, 0:128, :]
    X[1, 16:144, :] = E[1, 0:128, :]
    X[1, 0:16, :] = E[0, 112:128, :]
    bank0 = E[0, 144:160, :].astype(F32)[:8]
    bank1 = E[1, 144:160, :].astype(F32)[:8]
    X[1, 144:160, :] = jnp.concatenate([bank0, bank1], axis=0).astype(BF16)
    tail_over.wait_recv()
    bank_over.wait_recv()
    X[0, 0:16, :] = L[0]
    X[0, 144:160, :] = jnp.concatenate([L[1].astype(F32)[:8], bank0], axis=0).astype(BF16)
    for k in range(4):
        cols = slice(256 * k, 256 * k + 256)
        block = X[:, :, cols].reshape(320, 256).astype(F32)
        block = jnp.concatenate([block, jnp.zeros((64, 256), F32)], axis=0)
        XT[cols, :] = block.T.astype(BF16)

    two_relayed[0] = relay_two(0, two[0])
    two[2] = ring_two(2, one_relayed[2])

    low = lax.broadcasted_iota(jnp.int32, (1, 128), 1) < 64

    def split_heads(dst, value, g, p):
        dst[g, p, 0:160, :] = jnp.where(low, value, 0.0).astype(BF16)
        dst[g, p, 160:320, :] = jnp.where(low, 0.0, value).astype(BF16)

    def project_keys(m, dst):
        rows = X[...].reshape(320, 1024)
        for n in range(2):
            w = W[m, :, :, :, :, 256 * n:256 * n + 256].reshape(1024, 256)
            out = mm(rows, w)
            for g in range(2):
                for p in range(2):
                    split_heads(dst, out[160 * g:160 * g + 160, 128 * p:128 * p + 128], g, 2 * n + p)

    finish(two_relayed[0])
    project_keys(KEY, K)

    two_relayed[1] = relay_two(1, two[1])
    two_relayed[2] = relay_two(2, two[2])
    two[3] = ring_two(3, one_relayed[3])
    finish(two_relayed[1])
    query_rows = E[:, 0:144, :].reshape(288, 1024)
    for n in range(2):
        w = W[QUERY, :, :, :, :, 256 * n:256 * n + 256].reshape(1024, 256)
        out = mm(query_rows, w).astype(BF16)
        for g in range(2):
            for p in range(2):
                Q[g, 2 * n + p] = out[144 * g:144 * g + 144, 128 * p:128 * p + 128]

    def attend(i, carry):
        g = lax.div(i, 4)
        p = lax.rem(i, 4)
        scores = lax.dot_general(
            K[g, p], Q[g, p], (((1,), (1,)), ((), ())), preferred_element_type=F32)
        for h in range(2):
            s = scores[160 * h:160 * h + 160] * 0.125 + bias[g]
            e = jnp.exp(s - jnp.max(s, axis=0, keepdims=True))
            total = jnp.sum(e, axis=0, keepdims=True)
            PT[g, p, 160 * h:160 * h + 160, :] = (e / total).astype(BF16)
        return carry

    lax.fori_loop(0, 8, attend, 0)

    finish(two_relayed[2])
    out_over = remote(W.at[OUT, pl.ds(2 * other, 2)], WO2.at[core], device(flip=True))
    out_here = local(W.at[OUT, pl.ds(2 * core, 2)], WO2.at[core])
    grads_over.wait_recv()
    out_here.wait()
    out_over.wait_recv()

    def live_of(g, shape):
        r = lax.broadcasted_iota(jnp.int32, shape, 0)
        at = jnp.where(r < 128, r // 16, r - 128)
        return jnp.where((2 * z + g) * 8 + at < lengths[0], 1.0, 0.0).astype(F32)

    for g in range(2):
        ga = jnp.zeros((144, 512), F32)
        for h in range(2):
            w = WO2[h].reshape(512, 512)
            ga = ga + lax.dot_general(
                U[g, h], w, (((1,), (1,)), ((), ())), preferred_element_type=F32)
        ga = (ga * live_of(g, (144, 1))).astype(BF16)
        for p in range(4):
            GA[g, p] = ga[:, 128 * p:128 * p + 128]

    for g in range(2):
        for p in range(4):
            both = mm(PT[g, p], GA[g, p])
            GV[160 * g:160 * g + 160, 128 * p:128 * p + 128] = jnp.where(
                low, both[0:160], both[160:320]).astype(BF16)
    GV[320:384, :] = jnp.zeros((64, 512), BF16)

    def grad_rows(i, carry):
        block = mm(XT[pl.ds(pl.multiple_of(i * 256, 256), 256), :], GV[...])
        G[i] = block.astype(BF16).reshape(4, 2, 32, 512)
        return carry

    lax.fori_loop(0, 4, grad_rows, 0)

    def a_to(d, s):
        return device(dy=s) if d == 0 else device(dx=s)

    def b_to(d, s):
        return device(dx=s) if d == 0 else device(dy=s)

    a_at = (y, x)
    b_at = (x, y)

    def g_part(d, a, h):
        return (a, pl.ds(2 * h, 2), 0) if d == 0 else (pl.ds(2 * h, 2), a, 1)

    ways = [(d, s) for s in (1, -1) for d in (0, 1)]
    half_of = {1: 0, -1: 1}
    a1, a2a, a2b = {}, {}, {}
    for d, s in ways:
        h = half_of[s]
        a1[d, s] = remote(G.at[g_part(d, wrap(a_at[d], 2), h)], RA1.at[d, h], a_to(d, s))
    for d, s in ways:
        h = half_of[s]
        a2b[d, s] = remote(G.at[g_part(d, wrap(a_at[d], s), 1 - h)], RA2B.at[d, h], a_to(d, s))
    for d, s in ways:
        h = half_of[s]
        a1[d, s].wait_recv()
        SA[d, h] = (G[g_part(d, wrap(a_at[d], s), h)].astype(F32) + RA1[d, h].astype(F32)).astype(BF16)
        a2a[d, s] = remote(SA.at[d, h], RA2A.at[d, h], a_to(d, s))

    two_relayed[3] = relay_two(3, two[3])

    b1, b2a, b2b = {}, {}, {}
    for d in range(2):
        for s in (1, -1):
            a2a[d, s].wait_recv()
            a2b[d, s].wait_recv()
        for h in range(2):
            total = (G[g_part(d, a_at[d], h)].astype(F32) + RA2A[d, h].astype(F32)
                     + RA2B[d, 1 - h].astype(F32))
            RF[d, 2 * h:2 * h + 2] = total.reshape(2, 2, 16, 512)
            RS[d, 2 * h:2 * h + 2] = total.astype(BF16).reshape(2, 2, 16, 512)
        for s in (1, -1):
            h = half_of[s]
            b1[d, s] = remote(RS.at[d, wrap(b_at[d], 2), h], RB1.at[d, h], b_to(d, s))
            b2b[d, s] = remote(RS.at[d, wrap(b_at[d], s), 1 - h], RB2B.at[d, h], b_to(d, s))
    for d, s in ways:
        h = half_of[s]
        b1[d, s].wait_recv()
        SB[d, h] = (RF[d, wrap(b_at[d], s), h] + RB1[d, h].astype(F32)).astype(BF16)
        b2a[d, s] = remote(SB.at[d, h], RB2A.at[d, h], b_to(d, s))
    for d in range(2):
        for s in (1, -1):
            b2a[d, s].wait_recv()
            b2b[d, s].wait_recv()
        for h in range(2):
            total = RF[d, b_at[d], h] + RB2A[d, h].astype(F32) + RB2B[d, 1 - h].astype(F32)
            T[2 * d + h] = total
            ZS[2 * d + h] = total.astype(BF16)

    z1 = [remote(ZS.at[wrap(place, k)], ZR.at[k - 1], device(quad_by=k)) for k in (1, 2, 3)]

    finish(two_relayed[3])
    project_keys(VALUE, V)

    for copy in z1:
        copy.wait_recv()
    part = T[place]
    for k in range(3):
        part = part + ZR[k].astype(F32)
    ZQ[quad] = part.astype(BF16)
    z2 = {s: remote(ZQ.at[quad], ZQ.at[quad], device(dz=4 * s)) for s in (1, -1)}

    def attended(i, carry):
        g = lax.div(i, 4)
        p = lax.rem(i, 4)
        ATT[g, p] = lax.dot_general(
            PT[g, p], V[g, p], (((0,), (0,)), ((), ())), preferred_element_type=F32).astype(BF16)
        return carry

    lax.fori_loop(0, 8, attended, 0)

    z3 = {}
    for s in (1, -1):
        z2[s].wait_recv()
        cols = pl.ds(256 * half_of[s], 256)
        ref = ZQ.at[wrap(quad, -s), :, cols]
        z3[s] = remote(ref, ref, device(dz=4 * s))

    def project(g, h):
        rows = jnp.concatenate([ATT[g, p] for p in range(4)], axis=1)
        return mm(rows, WO2[h].reshape(512, 512))

    for h in range(2):
        PP[h] = project(other, h).astype(BF16)
    projected_over = remote(PP, PPR, device(flip=True))

    for s in (1, -1):
        z3[s].wait_recv()
    done = ((ZQ[0].astype(F32) + ZQ[1].astype(F32)) + ZQ[2].astype(F32)) + ZQ[3].astype(F32)
    OB[core, place] = done.astype(BF16)
    mine = OB.at[core, place]
    z4 = [remote(mine, mine, device(quad_by=k)) for k in (1, 2, 3)]
    z4 += [remote(mine, mine, device(quad_by=k, flip=True)) for k in (0, 1, 2, 3)]

    projected_over.wait_recv()
    live = live_of(core, (144, 1))
    for h in range(2):
        cols = slice(512 * h, 512 * h + 512)
        out = (project(core, h) + PPR[h].astype(F32)) * live
        fo_v[:, cols] = (fin[:, cols].astype(F32) + out[0:128]).astype(BF16)
        mo_v[:, cols] = out[128:136].astype(BF16)
    put_frames = local(fo_v, frames_out)
    put_memory = local(mo_v, memory_out)

    for copy in z4:
        copy.wait_recv()
    for h in range(2):
        value_grad[:, 512 * h:512 * h + 512] = OB[h].astype(F32).reshape(64, 512)
    put_frames.wait()
    put_memory.wait()
    for copy in sent:
        copy.wait_send()


def on_device(
    frames, memory_in, lengths, ln_gain, w_query, w_key, w_value, w_out, grad_frames, grad_memory
):
    any_spec = pl.BlockSpec(memory_space=pl.ANY)
    vmem = pltpu.VMEM
    scratch = [
        vmem((4, 4, 4, 2, 32, 512), BF16),
        vmem((2, 2, 4, 2, 32, 512), BF16),
        vmem((128, 1024), BF16),
        vmem((128, 1024), BF16),
        vmem((8, 1024), BF16),
        vmem((8, 1024), BF16),
        vmem((2, 160, 1024), BF16),
        vmem((2, 2, 144, 512), BF16),
        vmem((2, 16, 1024), BF16),
        vmem((2, 160, 1024), BF16),
        vmem((1024, 384), BF16),
        vmem((2, 160, 144), F32),
        vmem((2, 4, 320, 128), BF16),
        vmem((2, 4, 144, 128), BF16),
        vmem((2, 4, 320, 128), BF16),
        vmem((2, 4, 320, 144), BF16),
        vmem((2, 4, 144, 128), BF16),
        vmem((384, 512), BF16),
        vmem((2, 4, 144, 128), BF16),
        vmem((2, 144, 512), BF16),
        vmem((2, 144, 512), BF16),
        vmem((4, 4, 2, 32, 512), BF16),
        vmem((2, 2, 2, 32, 512), BF16),
        vmem((2, 2, 2, 32, 512), BF16),
        vmem((2, 2, 2, 32, 512), BF16),
        vmem((2, 2, 2, 32, 512), BF16),
        vmem((2, 4, 2, 16, 512), BF16),
        vmem((2, 4, 2, 16, 512), F32),
        vmem((2, 2, 16, 512), BF16),
        vmem((2, 2, 16, 512), BF16),
        vmem((2, 2, 16, 512), BF16),
        vmem((2, 2, 16, 512), BF16),
        vmem((4, 16, 512), F32),
        vmem((4, 16, 512), BF16),
        vmem((3, 16, 512), BF16),
        vmem((4, 16, 512), BF16),
        vmem((2, 4, 16, 512), BF16),
        vmem((128, 1024), BF16),
        vmem((8, 1024), BF16),
        vmem((1, 1024), F32),
        pltpu.SemaphoreType.DMA((N_REMOTE,)),
        pltpu.SemaphoreType.DMA((N_REMOTE,)),
        pltpu.SemaphoreType.DMA((N_LOCAL,)),
    ]
    frames_out, memory_out, value_grad = pl.pallas_call(
        kernel,
        out_shape=(
            jax.ShapeDtypeStruct((128, 1024), BF16),
            jax.ShapeDtypeStruct((8, 1024), BF16),
            jax.ShapeDtypeStruct((64, 1024), F32),
        ),
        in_specs=[any_spec, any_spec, pl.BlockSpec(memory_space=pltpu.SMEM)] + [any_spec] * 7,
        out_specs=(any_spec, any_spec, pl.BlockSpec(memory_space=vmem)),
        scratch_shapes=scratch,
        compiler_params=pltpu.CompilerParams(
            collective_id=0, has_side_effects=True, vmem_limit_bytes=48 * 1024 * 1024
        ),
    )(
        frames.reshape(128, 1024), memory_in.reshape(8, 1024), lengths, ln_gain.reshape(1, 1024),
        w_query, w_key, w_value, w_out,
        grad_frames.reshape(128, 1024), grad_memory.reshape(8, 1024),
    )
    return (frames_out.reshape(frames.shape), memory_out.reshape(memory_in.shape), value_grad)


def solution(mesh):
    return jax.shard_map(
        on_device,
        mesh=mesh,
        in_specs=(
            P("fsdp", "seg", None, None),
            P("fsdp", "seg", None),
            P("fsdp"),
            P(),
            P("fsdp", None),
            P("fsdp", None),
            P("fsdp", None),
            P("fsdp", None),
            P("fsdp", "seg", None, None),
            P("fsdp", "seg", None),
        ),
        out_specs=(P("fsdp", "seg", None, None), P("fsdp", "seg", None), P("fsdp", None)),
        check_vma=False,
    )
```

time: 569 us -> 88.1 us (0.15)
  waiting for transfers between devices: 498 us -> 0 us
  Pallas kernels: 0 us -> 76.7 us
  matrix products: 28.6 us -> 0 us
  between operations: 15.1 us -> 1.31 us
  other arithmetic: 7.43 us -> 0 us
  starting transfers between devices: 7.26 us -> 0 us
    all_gather x4 -> x0, waiting for transfers between devices: 213 us -> none  [the longest x1 60.3 us: on_device(): lax.all_gather(w_out, 'fsdp', axis=0, tiled=True)]
    psum x1 -> x0, waiting for transfers between devices: 202 us -> none  [on_device(): value_grad = lax.psum(grad_part, 'seg').astype(jnp.float32)]
    reduce_scatter x1 -> x0, waiting for transfers between devices: 78.8 us -> none  [on_device(): lax.psum_scatter(lax.dot_general(columns, grad_values, (((0,), (0,)), (()...]
    pallas_call x0 -> x1, Pallas kernels: none -> 76.7 us  [on_device(): pl.pallas_call(kernel, out_shape=(jax.ShapeDtypeStruct((128, 1024), BF16)...]
    dot_general x9 -> x0, matrix products: 28.6 us -> none  [the longest x1 6.95 us: on_device(): jnp.einsum('uthqk,utqhd->utkhd', soft_weights, grad_attended, preferred_e...]
    unnamed x21, local copies, waits for them, and re-layouts: 1.61 us -> 9.64 us
    ppermute x2 -> x0, starting transfers between devices: 6.84 us -> none  [passed_along(): return lax.ppermute(array, axis, pairs)]
    another operation x6 -> x0, local copies, waits for them, and re-layouts: 6.16 us -> none
  transfers between devices with their start and end apart: 8 -> 0, of which waited for: 7 -> 0; matrix products, arithmetic and copies ran while one was open for 8% -> 0% of each run, Pallas kernels for 0% -> 0%
where the time goes in v1:
time: 88.1 us; the launch traced here: 87.7 us
  Pallas kernels  76.7 us (87%)
  local copies, waits for them, and re-layouts  9.64 us (11%)
  between operations  1.31 us (1%)
    pallas_call x1, Pallas kernels, on_device(): pl.pallas_call(kernel, out_shape=(jax.ShapeDtypeStruct((128, 1024), BF16)...  76.7 us
    unnamed x21, local copies, waits for them, and re-layouts  9.64 us

profile of v1, /device:TPU:1, one launch (start us, length us, event | category | flops | bytes accessed | tf_op | source)
XLA Modules:
  0.0 87.7 jit_solution(7286674338411624856)
XLA Ops:
  1.3 0.0 copy-start.8
  1.3 0.7 copy-done.8
  2.0 0.0 copy-start
  2.0 0.9 %copy-done = bf16[1,8,16,1024]{3,2,1,0:T(8,128)(2,1)S(1)} copy-done((bf16[1,8,16,1024]{3,2,1,0:T(8,128)(2,1)S(1)}, bf16[1,8,16,1024]{3,2,1,0:T(8,128)(2,1)}, u32[]{:S(2)}) %copy-start) | copy-done | bytes 262168
  2.9 0.0 copy-start.1
  2.9 0.9 %copy-done.1 = bf16[1,8,16,1024]{3,2,1,0:T(8,128)(2,1)S(1)} copy-done((bf16[1,8,16,1024]{3,2,1,0:T(8,128)(2,1)S(1)}, bf16[1,8,16,1024]{3,2,1,0:T(8,128)(2,1)}, u32[]{:S(2)}) %copy-start.1) | copy-done | bytes 262168
  3.9 0.0 copy-start.2
  3.9 0.9 %copy-done.2 = bf16[64,1024]{1,0:T(8,128)(2,1)S(1)} copy-done((bf16[64,1024]{1,0:T(8,128)(2,1)S(1)}, bf16[64,1024]{1,0:T(8,128)(2,1)}, u32[]{:S(2)}) %copy-start.2) | copy-done | bytes 131096
  4.8 0.0 copy-start.3
  4.8 0.9 %copy-done.3 = bf16[64,1024]{1,0:T(8,128)(2,1)S(1)} copy-done((bf16[64,1024]{1,0:T(8,128)(2,1)S(1)}, bf16[64,1024]{1,0:T(8,128)(2,1)}, u32[]{:S(2)}) %copy-start.3) | copy-done | bytes 131096
  5.7 0.0 copy-start.4
  5.7 0.9 %copy-done.4 = bf16[64,1024]{1,0:T(8,128)(2,1)S(1)} copy-done((bf16[64,1024]{1,0:T(8,128)(2,1)S(1)}, bf16[64,1024]{1,0:T(8,128)(2,1)}, u32[]{:S(2)}) %copy-start.4) | copy-done | bytes 131096
  6.6 0.0 copy-start.5
  6.6 0.9 %copy-done.5 = bf16[64,1024]{1,0:T(8,128)(2,1)S(1)} copy-done((bf16[64,1024]{1,0:T(8,128)(2,1)S(1)}, bf16[64,1024]{1,0:T(8,128)(2,1)}, u32[]{:S(2)}) %copy-start.5) | copy-done | bytes 131096
  7.5 0.0 copy-start.6
  7.5 0.7 copy-done.6
  8.2 0.0 copy-start.7
  8.2 0.7 copy-done.7
  8.9 76.7 %shard_map.121 = (bf16[128,1024]{1,0:T(8,128)(2,1)S(1)}, bf16[8,1024]{1,0:T(8,128)(2,1)S(1)}, f32[64,1024]{1,0:T(8,128)S(1)}) custom-call(bf16[128,1024]{1,0:T(8,128)(2,1)S(1)} %bitcast.8, bf16[8,1024]{1,0:T(8,128)(2,1)S(1)} %bitcast.10, s32[1]{0:T(128)S(6)} %copy.16.lengths, f32[1,1024]{1,0:T(1,128)S(1)} %bitcast.13, bf16[64,1024]{1,0:T(8,128)(2,1)S(1)} %copy-done.2, ...), custom_call_target="tpu_custom_call" | custom-call | tf_op jit(solution)/shard_map/pallas_call | solution.py:473
  85.7 0.7 copy.17
  86.4 0.6 copy.18
  87.0 0.7 copy.19
Async XLA Ops:
  1.3 0.7 copy-start.8
  2.0 0.9 %copy-start = (bf16[1,8,16,1024]{3,2,1,0:T(8,128)(2,1)S(1)}, bf16[1,8,16,1024]{3,2,1,0:T(8,128)(2,1)}, u32[]{:S(2)}) copy-start(bf16[1,8,16,1024]{3,2,1,0:T(8,128)(2,1)} %param.10) | copy-start | bytes 786436
  2.9 0.9 %copy-start.1 = (bf16[1,8,16,1024]{3,2,1,0:T(8,128)(2,1)S(1)}, bf16[1,8,16,1024]{3,2,1,0:T(8,128)(2,1)}, u32[]{:S(2)}) copy-start(bf16[1,8,16,1024]{3,2,1,0:T(8,128)(2,1)} %param.18) | copy-start | bytes 786436
  3.9 0.9 %copy-start.2 = (bf16[64,1024]{1,0:T(8,128)(2,1)S(1)}, bf16[64,1024]{1,0:T(8,128)(2,1)}, u32[]{:S(2)}) copy-start(bf16[64,1024]{1,0:T(8,128)(2,1)} %w_query.1) | copy-start | bytes 393220
  4.8 0.9 %copy-start.3 = (bf16[64,1024]{1,0:T(8,128)(2,1)S(1)}, bf16[64,1024]{1,0:T(8,128)(2,1)}, u32[]{:S(2)}) copy-start(bf16[64,1024]{1,0:T(8,128)(2,1)} %w_key.1) | copy-start | bytes 393220
  5.7 0.9 %copy-start.4 = (bf16[64,1024]{1,0:T(8,128)(2,1)S(1)}, bf16[64,1024]{1,0:T(8,128)(2,1)}, u32[]{:S(2)}) copy-start(bf16[64,1024]{1,0:T(8,128)(2,1)} %w_value.1) | copy-start | bytes 393220
  6.6 0.9 %copy-start.5 = (bf16[64,1024]{1,0:T(8,128)(2,1)S(1)}, bf16[64,1024]{1,0:T(8,128)(2,1)}, u32[]{:S(2)}) copy-start(bf16[64,1024]{1,0:T(8,128)(2,1)} %w_out.1) | copy-start | bytes 393220
  7.5 0.7 copy-start.6
  8.2 0.7 copy-start.7

commit v2 on v1

--- a/solution.py
+++ b/solution.py
@@ -12,9 +12,9 @@
 MESH = pl.DeviceIdType.MESH
 EPSILON = 1e-05
 MASKED = -1e30
-KEY, QUERY, OUT, VALUE = 0, 1, 2, 3
+OUT, KEY, QUERY, VALUE = 0, 1, 2, 3
 N_REMOTE = 120
-N_LOCAL = 16
+N_LOCAL = 20
 
 
 def mm(a, b):
@@ -23,11 +23,10 @@
 
 def kernel(
     frames, memory, lengths, gain, w_query, w_key, w_value, w_out, grad_frames, grad_memory,
-    frames_out, memory_out, value_grad,
-    W, WO2, fin, gin, mem, gmem, E, U, L, X, XT, bias, K, Q, V, PT, GA, GV, ATT, PP, PPR,
-    G, RA1, RA2A, RA2B, SA, RS, RF, RB1, RB2A, RB2B, SB, T, ZS, ZR, ZQ, OB,
-    fo_v, mo_v, gain_v,
-    send_sem, recv_sem, local_sem,
+    fo_v, mo_v, vg_v,
+    W, WO2, fin, mem, gmem, E, U, L, X, XT, bias, K, Q, V, PT, GA, GV, ATT, PP, PPR,
+    G, RA1, RA2A, RA2B, SA, RS, RF, RZ, ZQ, OB, gain_v,
+    send_sem, recv_sem, local_sem, token_sem,
 ):
     seg = lax.axis_index("seg")
     fsdp = lax.axis_index("fsdp")
@@ -73,7 +72,7 @@
         copy.start()
         return copy
 
-    weights = (w_key, w_query, w_out, w_value)
+    weights = (w_out, w_key, w_query, w_value)
     own_columns = pl.ds(pl.multiple_of(core * 512, 512), 512)
     own = []
     for m in range(4):
@@ -84,17 +83,24 @@
     in_frames = local(frames, fin)
     in_gain = local(gain, gain_v)
     in_mem = local(memory, mem)
-    in_grad = local(grad_frames, gin)
     in_gmem = local(grad_memory, gmem)
-
-    partners = [device(dx=1), device(dx=-1), device(dy=1), device(dy=-1), device(flip=True)]
-    partners += [device(dz=1), device(dz=-1), device(dz=4), device(dz=-4)]
-    for k in (1, 2, 3):
-        partners += [device(quad_by=k), device(quad_by=k, flip=True)]
+    in_grad = [local(grad_frames.at[:, pl.ds(512 * h, 512)], U.at[core, h, pl.ds(0, 128)])
+               for h in range(2)]
+
+    partners = [device(dx=1), device(dx=-1), device(dy=1), device(dy=-1), device(flip=True),
+                device(dz=1), device(dz=-1)]
     barrier = pltpu.get_barrier_semaphore()
     for partner in partners:
         pl.semaphore_signal(barrier, inc=1, device_id=partner, device_id_type=MESH)
     pl.semaphore_wait(barrier, len(partners))
+
+    def pass_word(r):
+        for i, s in enumerate((1, -1)):
+            if r > 0:
+                pl.semaphore_wait(token_sem.at[r - 1, i], 1)
+            if r < 4:
+                pl.semaphore_signal(token_sem.at[r, i], inc=1, device_id=device(dz=s),
+                                    device_id_type=MESH)
 
     def first_to(d, s):
         return device(dx=s) if d == 0 else device(dy=s)
@@ -148,10 +154,14 @@
         return W[m].reshape(1024, 512)
 
     one, one_relayed, two, two_relayed = {}, {}, {}, {}
-    for m in range(4):
+
+    def begin(m):
         for copy in own[m]:
             copy.wait()
         one[m] = ring_one(m)
+
+    for m in (OUT, KEY, QUERY):
+        begin(m)
 
     in_frames.wait()
     in_gain.wait()
@@ -169,20 +179,18 @@
     E[core, 144:160, :] = jnp.concatenate([mem[...].astype(F32), zeros8], axis=0).astype(BF16)
     rows_over = remote(E.at[core], E.at[core], device(flip=True))
 
-    for m in range(4):
+    for m in (OUT, KEY, QUERY):
         one_relayed[m] = relay_one(m, one[m])
 
-    in_grad.wait()
     in_gmem.wait()
     for h in range(2):
-        cols = slice(512 * h, 512 * h + 512)
-        U[core, h, 0:128, :] = gin[:, cols]
+        in_grad[h].wait()
         U[core, h, 128:144, :] = jnp.concatenate(
-            [gmem[:, cols].astype(F32), zeros8[:, :512]], axis=0).astype(BF16)
+            [gmem[:, 512 * h:512 * h + 512].astype(F32), zeros8[:, :512]], axis=0).astype(BF16)
     grads_over = remote(U.at[core], U.at[core], device(flip=True))
 
-    two[0] = ring_two(0, one_relayed[0])
-    two[1] = ring_two(1, one_relayed[1])
+    two[OUT] = ring_two(OUT, one_relayed[OUT])
+    two[KEY] = ring_two(KEY, one_relayed[KEY])
     rows_over.wait_recv()
     tail_over = remote(E.at[1, 112:128], L.at[0], device(dz=1))
     bank_over = remote(E.at[1, 144:160], L.at[1], device(dz=1))
@@ -205,18 +213,48 @@
     bank0 = E[0, 144:160, :].astype(F32)[:8]
     bank1 = E[1, 144:160, :].astype(F32)[:8]
     X[1, 144:160, :] = jnp.concatenate([bank0, bank1], axis=0).astype(BF16)
+
+    two_relayed[OUT] = relay_two(OUT, two[OUT])
+    two[QUERY] = ring_two(QUERY, one_relayed[QUERY])
+    begin(VALUE)
+
     tail_over.wait_recv()
     bank_over.wait_recv()
     X[0, 0:16, :] = L[0]
     X[0, 144:160, :] = jnp.concatenate([L[1].astype(F32)[:8], bank0], axis=0).astype(BF16)
     for k in range(4):
-        cols = slice(256 * k, 256 * k + 256)
-        block = X[:, :, cols].reshape(320, 256).astype(F32)
-        block = jnp.concatenate([block, jnp.zeros((64, 256), F32)], axis=0)
-        XT[cols, :] = block.T.astype(BF16)
-
-    two_relayed[0] = relay_two(0, two[0])
-    two[2] = ring_two(2, one_relayed[2])
+        block = X[:, :, 256 * k:256 * k + 256].reshape(320, 256).astype(F32)
+        block = jnp.concatenate([block, jnp.zeros((64, 256), F32)], axis=0).T.astype(BF16)
+        for i in range(4):
+            XT[0, k, i] = block[64 * i:64 * i + 32]
+            XT[1, i, k] = block[64 * i + 32:64 * i + 64]
+
+    finish(two_relayed[OUT])
+    pass_word(0)
+    out_over = remote(W.at[OUT, pl.ds(2 * other, 2)], WO2.at[core], device(flip=True))
+    out_here = local(W.at[OUT, pl.ds(2 * core, 2)], WO2.at[core])
+    two_relayed[KEY] = relay_two(KEY, two[KEY])
+    one_relayed[VALUE] = relay_one(VALUE, one[VALUE])
+    pass_word(1)
+
+    def live_of(g, shape):
+        r = lax.broadcasted_iota(jnp.int32, shape, 0)
+        at = jnp.where(r < 128, r // 16, r - 128)
+        return jnp.where((2 * z + g) * 8 + at < lengths[0], 1.0, 0.0).astype(F32)
+
+    grads_over.wait_recv()
+    out_here.wait()
+    out_over.wait_recv()
+    for g in range(2):
+        ga = jnp.zeros((144, 512), F32)
+        for h in range(2):
+            w = WO2[h].reshape(512, 512)
+            ga = ga + lax.dot_general(
+                U[g, h], w, (((1,), (1,)), ((), ())), preferred_element_type=F32)
+        ga = (ga * live_of(g, (144, 1))).astype(BF16)
+        for p in range(4):
+            GA[g, p] = ga[:, 128 * p:128 * p + 128]
+    pass_word(2)
 
     low = lax.broadcasted_iota(jnp.int32, (1, 128), 1) < 64
 
@@ -233,13 +271,12 @@
                 for p in range(2):
                     split_heads(dst, out[160 * g:160 * g + 160, 128 * p:128 * p + 128], g, 2 * n + p)
 
-    finish(two_relayed[0])
+    two_relayed[QUERY] = relay_two(QUERY, two[QUERY])
+    finish(two_relayed[KEY])
     project_keys(KEY, K)
-
-    two_relayed[1] = relay_two(1, two[1])
-    two_relayed[2] = relay_two(2, two[2])
-    two[3] = ring_two(3, one_relayed[3])
-    finish(two_relayed[1])
+    pass_word(3)
+    two[VALUE] = ring_two(VALUE, one_relayed[VALUE])
+    finish(two_relayed[QUERY])
     query_rows = E[:, 0:144, :].reshape(288, 1024)
     for n in range(2):
         w = W[QUERY, :, :, :, :, 256 * n:256 * n + 256].reshape(1024, 256)
@@ -262,28 +299,7 @@
 
     lax.fori_loop(0, 8, attend, 0)
 
-    finish(two_relayed[2])
-    out_over = remote(W.at[OUT, pl.ds(2 * other, 2)], WO2.at[core], device(flip=True))
-    out_here = local(W.at[OUT, pl.ds(2 * core, 2)], WO2.at[core])
-    grads_over.wait_recv()
-    out_here.wait()
-    out_over.wait_recv()
-
-    def live_of(g, shape):
-        r = lax.broadcasted_iota(jnp.int32, shape, 0)
-        at = jnp.where(r < 128, r // 16, r - 128)
-        return jnp.where((2 * z + g) * 8 + at < lengths[0], 1.0, 0.0).astype(F32)
-
-    for g in range(2):
-        ga = jnp.zeros((144, 512), F32)
-        for h in range(2):
-            w = WO2[h].reshape(512, 512)
-            ga = ga + lax.dot_general(
-                U[g, h], w, (((1,), (1,)), ((), ())), preferred_element_type=F32)
-        ga = (ga * live_of(g, (144, 1))).astype(BF16)
-        for p in range(4):
-            GA[g, p] = ga[:, 128 * p:128 * p + 128]
-
+    pass_word(4)
     for g in range(2):
         for p in range(4):
             both = mm(PT[g, p], GA[g, p])
@@ -291,80 +307,74 @@
                 low, both[0:160], both[160:320]).astype(BF16)
     GV[320:384, :] = jnp.zeros((64, 512), BF16)
 
-    def grad_rows(i, carry):
-        block = mm(XT[pl.ds(pl.multiple_of(i * 256, 256), 256), :], GV[...])
-        G[i] = block.astype(BF16).reshape(4, 2, 32, 512)
-        return carry
-
-    lax.fori_loop(0, 4, grad_rows, 0)
-
     def a_to(d, s):
         return device(dy=s) if d == 0 else device(dx=s)
 
-    def b_to(d, s):
-        return device(dx=s) if d == 0 else device(dy=s)
-
     a_at = (y, x)
     b_at = (x, y)
-
-    def g_part(d, a, h):
-        return (a, pl.ds(2 * h, 2), 0) if d == 0 else (pl.ds(2 * h, 2), a, 1)
-
     ways = [(d, s) for s in (1, -1) for d in (0, 1)]
     half_of = {1: 0, -1: 1}
+
+    def g_part(d, by, h):
+        return (d, wrap(a_at[d], by), pl.ds(2 * h, 2))
+
     a1, a2a, a2b = {}, {}, {}
-    for d, s in ways:
-        h = half_of[s]
-        a1[d, s] = remote(G.at[g_part(d, wrap(a_at[d], 2), h)], RA1.at[d, h], a_to(d, s))
-    for d, s in ways:
-        h = half_of[s]
-        a2b[d, s] = remote(G.at[g_part(d, wrap(a_at[d], s), 1 - h)], RA2B.at[d, h], a_to(d, s))
+    for by in (2, 1, -1, 0):
+        rows = jnp.concatenate(
+            [XT[d, wrap(a_at[d], by)].reshape(128, 384) for d in range(2)], axis=0)
+        block = mm(rows, GV[...]).astype(BF16)
+        for d in range(2):
+            G[d, wrap(a_at[d], by)] = block[128 * d:128 * d + 128].reshape(4, 32, 512)
+        if by == 2:
+            for d, s in ways:
+                h = half_of[s]
+                a1[d, s] = remote(G.at[g_part(d, 2, h)], RA1.at[d, h], a_to(d, s))
+        elif by != 0:
+            for d in range(2):
+                h = half_of[by]
+                a2b[d, by] = remote(G.at[g_part(d, by, 1 - h)], RA2B.at[d, h], a_to(d, by))
     for d, s in ways:
         h = half_of[s]
         a1[d, s].wait_recv()
-        SA[d, h] = (G[g_part(d, wrap(a_at[d], s), h)].astype(F32) + RA1[d, h].astype(F32)).astype(BF16)
+        SA[d, h] = (G[g_part(d, s, h)].astype(F32) + RA1[d, h].astype(F32)).astype(BF16)
         a2a[d, s] = remote(SA.at[d, h], RA2A.at[d, h], a_to(d, s))
 
-    two_relayed[3] = relay_two(3, two[3])
-
-    b1, b2a, b2b = {}, {}, {}
+    two_relayed[VALUE] = relay_two(VALUE, two[VALUE])
+
     for d in range(2):
         for s in (1, -1):
             a2a[d, s].wait_recv()
             a2b[d, s].wait_recv()
         for h in range(2):
-            total = (G[g_part(d, a_at[d], h)].astype(F32) + RA2A[d, h].astype(F32)
+            total = (G[g_part(d, 0, h)].astype(F32) + RA2A[d, h].astype(F32)
                      + RA2B[d, 1 - h].astype(F32))
             RF[d, 2 * h:2 * h + 2] = total.reshape(2, 2, 16, 512)
             RS[d, 2 * h:2 * h + 2] = total.astype(BF16).reshape(2, 2, 16, 512)
-        for s in (1, -1):
-            h = half_of[s]
-            b1[d, s] = remote(RS.at[d, wrap(b_at[d], 2), h], RB1.at[d, h], b_to(d, s))
-            b2b[d, s] = remote(RS.at[d, wrap(b_at[d], s), 1 - h], RB2B.at[d, h], b_to(d, s))
-    for d, s in ways:
-        h = half_of[s]
-        b1[d, s].wait_recv()
-        SB[d, h] = (RF[d, wrap(b_at[d], s), h] + RB1[d, h].astype(F32)).astype(BF16)
-        b2a[d, s] = remote(SB.at[d, h], RB2A.at[d, h], b_to(d, s))
-    for d in range(2):
-        for s in (1, -1):
-            b2a[d, s].wait_recv()
-            b2b[d, s].wait_recv()
-        for h in range(2):
-            total = RF[d, b_at[d], h] + RB2A[d, h].astype(F32) + RB2B[d, 1 - h].astype(F32)
-            T[2 * d + h] = total
-            ZS[2 * d + h] = total.astype(BF16)
-
-    z1 = [remote(ZS.at[wrap(place, k)], ZR.at[k - 1], device(quad_by=k)) for k in (1, 2, 3)]
-
-    finish(two_relayed[3])
+
+    z1 = []
+    for k in (2, 1, 3, 0):
+        to_place = wrap(place, k)
+        d = lax.div(to_place, 2)
+        for o in (2, 1, 3, 0):
+            if o == 0 and k == 0:
+                continue
+            along = x + d * (y - x)
+            to_x = wrap(x, (1 - d) * o)
+            to_y = wrap(y, d * o)
+            to = ((quad * 4 + to_place) * 2 + core, to_y * 4 + to_x)
+            z1.append(remote(RS.at[d, wrap(along, o), lax.rem(to_place, 2)], RZ.at[o, k], to))
+
+    finish(two_relayed[VALUE])
     project_keys(VALUE, V)
 
     for copy in z1:
         copy.wait_recv()
-    part = T[place]
-    for k in range(3):
-        part = part + ZR[k].astype(F32)
+    own_d = lax.div(place, 2)
+    part = RF[own_d, x + own_d * (y - x), lax.rem(place, 2)]
+    for o in range(4):
+        for k in range(4):
+            if o or k:
+                part = part + RZ[o, k].astype(F32)
     ZQ[quad] = part.astype(BF16)
     z2 = {s: remote(ZQ.at[quad], ZQ.at[quad], device(dz=4 * s)) for s in (1, -1)}
 
@@ -407,28 +417,37 @@
         out = (project(core, h) + PPR[h].astype(F32)) * live
         fo_v[:, cols] = (fin[:, cols].astype(F32) + out[0:128]).astype(BF16)
         mo_v[:, cols] = out[128:136].astype(BF16)
-    put_frames = local(fo_v, frames_out)
-    put_memory = local(mo_v, memory_out)
 
     for copy in z4:
         copy.wait_recv()
     for h in range(2):
-        value_grad[:, 512 * h:512 * h + 512] = OB[h].astype(F32).reshape(64, 512)
-    put_frames.wait()
-    put_memory.wait()
+        vg_v[:, 512 * h:512 * h + 512] = OB[h].astype(F32).reshape(64, 512)
     for copy in sent:
         copy.wait_send()
+
+
+def hand_out(fo_v, mo_v, vg_v, frames_out, memory_out, value_grad, sem):
+    copies = [
+        pltpu.make_async_copy(fo_v, frames_out, sem.at[0]),
+        pltpu.make_async_copy(mo_v, memory_out, sem.at[1]),
+        pltpu.make_async_copy(vg_v, value_grad, sem.at[2]),
+    ]
+    for copy in copies:
+        copy.start()
+    for copy in copies:
+        copy.wait()
 
 
 def on_device(
     frames, memory_in, lengths, ln_gain, w_query, w_key, w_value, w_out, grad_frames, grad_memory
 ):
+    hbm = pl.BlockSpec(memory_space=pltpu.HBM)
+    place = functools.partial(pltpu.with_memory_space_constraint, memory_space=pltpu.HBM)
     any_spec = pl.BlockSpec(memory_space=pl.ANY)
     vmem = pltpu.VMEM
     scratch = [
         vmem((4, 4, 4, 2, 32, 512), BF16),
         vmem((2, 2, 4, 2, 32, 512), BF16),
-        vmem((128, 1024), BF16),
         vmem((128, 1024), BF16),
         vmem((8, 1024), BF16),
         vmem((8, 1024), BF16),
@@ -436,7 +455,7 @@
         vmem((2, 2, 144, 512), BF16),
         vmem((2, 16, 1024), BF16),
         vmem((2, 160, 1024), BF16),
-        vmem((1024, 384), BF16),
+        vmem((2, 4, 4, 32, 384), BF16),
         vmem((2, 160, 144), F32),
         vmem((2, 4, 320, 128), BF16),
         vmem((2, 4, 144, 128), BF16),
@@ -447,47 +466,49 @@
         vmem((2, 4, 144, 128), BF16),
         vmem((2, 144, 512), BF16),
         vmem((2, 144, 512), BF16),
-        vmem((4, 4, 2, 32, 512), BF16),
+        vmem((2, 4, 4, 32, 512), BF16),
         vmem((2, 2, 2, 32, 512), BF16),
         vmem((2, 2, 2, 32, 512), BF16),
         vmem((2, 2, 2, 32, 512), BF16),
         vmem((2, 2, 2, 32, 512), BF16),
         vmem((2, 4, 2, 16, 512), BF16),
         vmem((2, 4, 2, 16, 512), F32),
-        vmem((2, 2, 16, 512), BF16),
-        vmem((2, 2, 16, 512), BF16),
-        vmem((2, 2, 16, 512), BF16),
-        vmem((2, 2, 16, 512), BF16),
-        vmem((4, 16, 512), F32),
-        vmem((4, 16, 512), BF16),
-        vmem((3, 16, 512), BF16),
+        vmem((4, 4, 16, 512), BF16),
         vmem((4, 16, 512), BF16),
         vmem((2, 4, 16, 512), BF16),
-        vmem((128, 1024), BF16),
-        vmem((8, 1024), BF16),
         vmem((1, 1024), F32),
         pltpu.SemaphoreType.DMA((N_REMOTE,)),
         pltpu.SemaphoreType.DMA((N_REMOTE,)),
         pltpu.SemaphoreType.DMA((N_LOCAL,)),
+        pltpu.SemaphoreType.REGULAR((4, 2)),
     ]
-    frames_out, memory_out, value_grad = pl.pallas_call(
+    shapes = (
+        jax.ShapeDtypeStruct((128, 1024), BF16),
+        jax.ShapeDtypeStruct((8, 1024), BF16),
+        jax.ShapeDtypeStruct((64, 1024), F32),
+    )
+    results = pl.pallas_call(
         kernel,
-        out_shape=(
-            jax.ShapeDtypeStruct((128, 1024), BF16),
-            jax.ShapeDtypeStruct((8, 1024), BF16),
-            jax.ShapeDtypeStruct((64, 1024), F32),
-        ),
-        in_specs=[any_spec, any_spec, pl.BlockSpec(memory_space=pltpu.SMEM)] + [any_spec] * 7,
-        out_specs=(any_spec, any_spec, pl.BlockSpec(memory_space=vmem)),
+        out_shape=shapes,
+        in_specs=[hbm, hbm, pl.BlockSpec(memory_space=pltpu.SMEM)] + [hbm] * 7,
+        out_specs=(pl.BlockSpec(memory_space=vmem),) * 3,
         scratch_shapes=scratch,
         compiler_params=pltpu.CompilerParams(
-            collective_id=0, has_side_effects=True, vmem_limit_bytes=48 * 1024 * 1024
+            collective_id=0, has_side_effects=True, vmem_limit_bytes=40 * 1024 * 1024
         ),
     )(
-        frames.reshape(128, 1024), memory_in.reshape(8, 1024), lengths, ln_gain.reshape(1, 1024),
-        w_query, w_key, w_value, w_out,
-        grad_frames.reshape(128, 1024), grad_memory.reshape(8, 1024),
+        place(frames.reshape(128, 1024)), place(memory_in.reshape(8, 1024)), lengths,
+        place(ln_gain.reshape(1, 1024)), place(w_query), place(w_key), place(w_value),
+        place(w_out), place(grad_frames.reshape(128, 1024)), place(grad_memory.reshape(8, 1024)),
     )
+    frames_out, memory_out, value_grad = pl.pallas_call(
+        hand_out,
+        out_shape=shapes,
+        in_specs=[any_spec] * 3,
+        out_specs=(any_spec,) * 3,
+        scratch_shapes=[pltpu.SemaphoreType.DMA((3,))],
+        compiler_params=pltpu.CompilerParams(vmem_limit_bytes=1024 * 1024),
+    )(*results)
     return (frames_out.reshape(frames.shape), memory_out.reshape(memory_in.shape), value_grad)
 
 

time: 88.1 us -> 76.6 us (0.87)
  local copies, waits for them, and re-layouts: 9.64 us -> 0 us
  Pallas kernels: 76.7 us -> 75.2 us
    unnamed x21 -> x0, local copies, waits for them, and re-layouts: 9.64 us -> none
    pallas_call x1 -> x2, Pallas kernels: 76.7 us -> 75.2 us  [the longest x1 74.3 us: on_device(): pl.pallas_call(kernel, out_shape=shapes, in_specs=[hbm, hbm, pl.BlockSpec...]
where the time goes in v2:
time: 76.6 us; the launch traced here: 76.4 us
  Pallas kernels  75.2 us (98%)
  between operations  1.29 us (2%)
    pallas_call x1, Pallas kernels, on_device(): pl.pallas_call(kernel, out_shape=shapes, in_specs=[hbm, hbm, pl.BlockSpec...  74.3 us

profile of v2, /device:TPU:1, one launch (start us, length us, event | category | flops | bytes accessed | tf_op | source)
XLA Modules:
  0.0 76.4 jit_solution(13154223656071810888)
XLA Ops:
  1.3 74.3 %shard_map.121 = (bf16[128,1024]{1,0:T(8,128)(2,1)S(1)}, bf16[8,1024]{1,0:T(8,128)(2,1)S(1)}, f32[64,1024]{1,0:T(8,128)S(1)}) custom-call(bf16[128,1024]{1,0:T(8,128)(2,1)} %bitcast.7, bf16[8,1024]{1,0:T(8,128)(2,1)} %bitcast.9, s32[1]{0:T(128)S(6)} %copy.13.lengths, f32[1,1024]{1,0:T(1,128)} %bitcast.11, bf16[64,1024]{1,0:T(8,128)(2,1)} %w_query.1, ...), custom_call_target="tpu_custom_call" | custom-call | tf_op jit(solution)/shard_map/pallas_call | solution.py:490
  75.6 0.8 %shard_map.122 = (bf16[128,1024]{1,0:T(8,128)(2,1)}, bf16[8,1024]{1,0:T(8,128)(2,1)}, f32[64,1024]{1,0:T(8,128)}) custom-call(bf16[128,1024]{1,0:T(8,128)(2,1)S(1)} %get-tuple-element.9.fo_v, bf16[8,1024]{1,0:T(8,128)(2,1)S(1)} %get-tuple-element.10.mo_v, f32[64,1024]{1,0:T(8,128)S(1)} %get-tuple-element.11.vg_v), custom_call_target="tpu_custom_call" | custom-call | tf_op jit(solution)/shard_map/pallas_call | solution.py:504

commit v3 on v2

--- a/solution.py
+++ b/solution.py
@@ -13,7 +13,7 @@
 EPSILON = 1e-05
 MASKED = -1e30
 OUT, KEY, QUERY, VALUE = 0, 1, 2, 3
-N_REMOTE = 120
+N_REMOTE = 192
 N_LOCAL = 20
 
 
@@ -108,60 +108,60 @@
     def second_to(d, s):
         return device(dy=s) if d == 0 else device(dx=s)
 
-    def ring_one(m):
-        return {(d, s): remote(W.at[m, y, x, d], W.at[m, y, x, d], first_to(d, s))
-                for s in (1, -1) for d in (0, 1)}
-
-    def relay_one(m, came):
-        out = {}
+    def piece(m, d, first=0, second=0, rows=None):
+        dx, dy = (first, second) if d == 0 else (second, first)
+        at = (m, wrap(y, dy), wrap(x, dx), d)
+        return W.at[at if rows is None else at + (rows,)]
+
+    flows = [(d, s) for s in (1, -1) for d in (0, 1)]
+    direct, halves, forwarded, relayed = {}, {}, {}, {}
+
+    def forward(m, d, kind):
         for s in (1, -1):
-            for d in (0, 1):
-                came[d, s].wait_recv()
-                rows = pl.ds(0 if s == 1 else 16, 16)
-                ref = (W.at[m, y, wrap(x, -s), 0, rows] if d == 0
-                       else W.at[m, wrap(y, -s), x, 1, rows])
-                out[d, s] = remote(ref, ref, first_to(d, s))
-        return out
-
-    def ring_two(m, came):
-        out = {}
+            ref = piece(m, d, first=kind)
+            forwarded[m, d, s, kind] = remote(ref, ref, second_to(d, s))
+
+    def stage0(m):
+        for copy in own[m]:
+            copy.wait()
+        for d, s in flows:
+            ref = piece(m, d)
+            direct[m, d, s] = remote(ref, ref, first_to(d, s))
+        for d in (0, 1):
+            forward(m, d, 0)
+
+    def stage1(m):
+        for d, s in flows:
+            direct[m, d, s].wait_recv()
+            ref = piece(m, d, first=-s, rows=pl.ds(0 if s == 1 else 16, 16))
+            halves[m, d, s] = remote(ref, ref, first_to(d, s))
+        for d, s in flows:
+            forward(m, d, -s)
+
+    def stage2(m):
         for d in (0, 1):
             for s in (1, -1):
-                came[d, s].wait_recv()
-        for s in (1, -1):
-            for d in (0, 1):
-                ref = W.at[m, y, :, 0] if d == 0 else W.at[m, :, x, 1]
-                out[d, s] = remote(ref, ref, second_to(d, s))
-        return out
-
-    def relay_two(m, came):
-        out = {}
-        for s in (1, -1):
-            for d in (0, 1):
-                came[d, s].wait_recv()
-                half = pl.ds(0 if s == 1 else 2, 2)
-                ref = (W.at[m, wrap(y, -s), half, 0] if d == 0
-                       else W.at[m, half, wrap(x, -s), 1])
-                out[d, s] = remote(ref, ref, second_to(d, s))
-        return out
-
-    def finish(came):
-        for s in (1, -1):
-            for d in (0, 1):
-                came[d, s].wait_recv()
-
-    def weight(m):
-        return W[m].reshape(1024, 512)
-
-    one, one_relayed, two, two_relayed = {}, {}, {}, {}
-
-    def begin(m):
-        for copy in own[m]:
-            copy.wait()
-        one[m] = ring_one(m)
+                halves[m, d, s].wait_recv()
+            forward(m, d, 2)
+
+    def stage3(m, kinds=(0, 1)):
+        for i in kinds:
+            for d, s in flows:
+                kind = ((0, -1), (1, 2))[(1 - s) // 2][i]
+                forwarded[m, d, s, kind].wait_recv()
+                ref = piece(m, d, first=kind, second=-s)
+                relayed[m, d, s, kind] = remote(ref, ref, second_to(d, s))
+
+    def stage4(m):
+        for d, s in flows:
+            for kind in ((1, 2), (0, -1))[(1 - s) // 2]:
+                forwarded[m, d, s, kind].wait_recv()
+        for d, s in flows:
+            for kind in ((0, -1), (1, 2))[(1 - s) // 2]:
+                relayed[m, d, s, kind].wait_recv()
 
     for m in (OUT, KEY, QUERY):
-        begin(m)
+        stage0(m)
 
     in_frames.wait()
     in_gain.wait()
@@ -180,7 +180,7 @@
     rows_over = remote(E.at[core], E.at[core], device(flip=True))
 
     for m in (OUT, KEY, QUERY):
-        one_relayed[m] = relay_one(m, one[m])
+        stage1(m)
 
     in_gmem.wait()
     for h in range(2):
@@ -189,8 +189,8 @@
             [gmem[:, 512 * h:512 * h + 512].astype(F32), zeros8[:, :512]], axis=0).astype(BF16)
     grads_over = remote(U.at[core], U.at[core], device(flip=True))
 
-    two[OUT] = ring_two(OUT, one_relayed[OUT])
-    two[KEY] = ring_two(KEY, one_relayed[KEY])
+    stage2(OUT)
+    stage2(KEY)
     rows_over.wait_recv()
     tail_over = remote(E.at[1, 112:128], L.at[0], device(dz=1))
     bank_over = remote(E.at[1, 144:160], L.at[1], device(dz=1))
@@ -214,9 +214,9 @@
     bank1 = E[1, 144:160, :].astype(F32)[:8]
     X[1, 144:160, :] = jnp.concatenate([bank0, bank1], axis=0).astype(BF16)
 
-    two_relayed[OUT] = relay_two(OUT, two[OUT])
-    two[QUERY] = ring_two(QUERY, one_relayed[QUERY])
-    begin(VALUE)
+    stage3(OUT)
+    stage2(QUERY)
+    stage3(KEY)
 
     tail_over.wait_recv()
     bank_over.wait_recv()
@@ -229,12 +229,12 @@
             XT[0, k, i] = block[64 * i:64 * i + 32]
             XT[1, i, k] = block[64 * i + 32:64 * i + 64]
 
-    finish(two_relayed[OUT])
+    stage4(OUT)
     pass_word(0)
     out_over = remote(W.at[OUT, pl.ds(2 * other, 2)], WO2.at[core], device(flip=True))
     out_here = local(W.at[OUT, pl.ds(2 * core, 2)], WO2.at[core])
-    two_relayed[KEY] = relay_two(KEY, two[KEY])
-    one_relayed[VALUE] = relay_one(VALUE, one[VALUE])
+    stage3(QUERY)
+    stage0(VALUE)
     pass_word(1)
 
     def live_of(g, shape):
@@ -242,6 +242,50 @@
         at = jnp.where(r < 128, r // 16, r - 128)
         return jnp.where((2 * z + g) * 8 + at < lengths[0], 1.0, 0.0).astype(F32)
 
+    low = lax.broadcasted_iota(jnp.int32, (1, 128), 1) < 64
+
+    def split_heads(dst, value, g, p):
+        dst[g, p, 0:160, :] = jnp.where(low, value, 0.0).astype(BF16)
+        dst[g, p, 160:320, :] = jnp.where(low, 0.0, value).astype(BF16)
+
+    def project_keys(m, dst):
+        rows = X[...].reshape(320, 1024)
+        for n in range(2):
+            w = W[m, :, :, :, :, 256 * n:256 * n + 256].reshape(1024, 256)
+            out = mm(rows, w)
+            for g in range(2):
+                for p in range(2):
+                    split_heads(dst, out[160 * g:160 * g + 160, 128 * p:128 * p + 128], g, 2 * n + p)
+
+    stage4(KEY)
+    project_keys(KEY, K)
+    pass_word(2)
+    stage1(VALUE)
+    stage4(QUERY)
+    query_rows = E[:, 0:144, :].reshape(288, 1024)
+    for n in range(2):
+        w = W[QUERY, :, :, :, :, 256 * n:256 * n + 256].reshape(1024, 256)
+        out = mm(query_rows, w).astype(BF16)
+        for g in range(2):
+            for p in range(2):
+                Q[g, 2 * n + p] = out[144 * g:144 * g + 144, 128 * p:128 * p + 128]
+
+    def attend(i, carry):
+        g = lax.div(i, 4)
+        p = lax.rem(i, 4)
+        scores = lax.dot_general(
+            K[g, p], Q[g, p], (((1,), (1,)), ((), ())), preferred_element_type=F32)
+        for h in range(2):
+            s = scores[160 * h:160 * h + 160] * 0.125 + bias[g]
+            e = jnp.exp(s - jnp.max(s, axis=0, keepdims=True))
+            total = jnp.sum(e, axis=0, keepdims=True)
+            PT[g, p, 160 * h:160 * h + 160, :] = (e / total).astype(BF16)
+        return carry
+
+    lax.fori_loop(0, 8, attend, 0)
+
+    pass_word(3)
+    stage2(VALUE)
     grads_over.wait_recv()
     out_here.wait()
     out_over.wait_recv()
@@ -254,51 +298,6 @@
         ga = (ga * live_of(g, (144, 1))).astype(BF16)
         for p in range(4):
             GA[g, p] = ga[:, 128 * p:128 * p + 128]
-    pass_word(2)
-
-    low = lax.broadcasted_iota(jnp.int32, (1, 128), 1) < 64
-
-    def split_heads(dst, value, g, p):
-        dst[g, p, 0:160, :] = jnp.where(low, value, 0.0).astype(BF16)
-        dst[g, p, 160:320, :] = jnp.where(low, 0.0, value).astype(BF16)
-
-    def project_keys(m, dst):
-        rows = X[...].reshape(320, 1024)
-        for n in range(2):
-            w = W[m, :, :, :, :, 256 * n:256 * n + 256].reshape(1024, 256)
-            out = mm(rows, w)
-            for g in range(2):
-                for p in range(2):
-                    split_heads(dst, out[160 * g:160 * g + 160, 128 * p:128 * p + 128], g, 2 * n + p)
-
-    two_relayed[QUERY] = relay_two(QUERY, two[QUERY])
-    finish(two_relayed[KEY])
-    project_keys(KEY, K)
-    pass_word(3)
-    two[VALUE] = ring_two(VALUE, one_relayed[VALUE])
-    finish(two_relayed[QUERY])
-    query_rows = E[:, 0:144, :].reshape(288, 1024)
-    for n in range(2):
-        w = W[QUERY, :, :, :, :, 256 * n:256 * n + 256].reshape(1024, 256)
-        out = mm(query_rows, w).astype(BF16)
-        for g in range(2):
-            for p in range(2):
-                Q[g, 2 * n + p] = out[144 * g:144 * g + 144, 128 * p:128 * p + 128]
-
-    def attend(i, carry):
-        g = lax.div(i, 4)
-        p = lax.rem(i, 4)
-        scores = lax.dot_general(
-            K[g, p], Q[g, p], (((1,), (1,)), ((), ())), preferred_element_type=F32)
-        for h in range(2):
-            s = scores[160 * h:160 * h + 160] * 0.125 + bias[g]
-            e = jnp.exp(s - jnp.max(s, axis=0, keepdims=True))
-            total = jnp.sum(e, axis=0, keepdims=True)
-            PT[g, p, 160 * h:160 * h + 160, :] = (e / total).astype(BF16)
-        return carry
-
-    lax.fori_loop(0, 8, attend, 0)
-
     pass_word(4)
     for g in range(2):
         for p in range(4):
@@ -339,7 +338,7 @@
         SA[d, h] = (G[g_part(d, s, h)].astype(F32) + RA1[d, h].astype(F32)).astype(BF16)
         a2a[d, s] = remote(SA.at[d, h], RA2A.at[d, h], a_to(d, s))
 
-    two_relayed[VALUE] = relay_two(VALUE, two[VALUE])
+    stage3(VALUE)
 
     for d in range(2):
         for s in (1, -1):
@@ -364,7 +363,7 @@
             to = ((quad * 4 + to_place) * 2 + core, to_y * 4 + to_x)
             z1.append(remote(RS.at[d, wrap(along, o), lax.rem(to_place, 2)], RZ.at[o, k], to))
 
-    finish(two_relayed[VALUE])
+    stage4(VALUE)
     project_keys(VALUE, V)
 
     for copy in z1:

time: 76.6 us -> 75 us (0.979)
  Pallas kernels: 75.2 us -> 73.5 us
    pallas_call x1, Pallas kernels: 74.3 us -> 72.7 us  [on_device(): pl.pallas_call(kernel, out_shape=shapes, in_specs=[hbm, hbm, pl.BlockSpec...]
where the time goes in v3:
time: 75 us; the launch traced here: 74.8 us
  Pallas kernels  73.5 us (98%)
  between operations  1.29 us (2%)
    pallas_call x1, Pallas kernels, on_device(): pl.pallas_call(kernel, out_shape=shapes, in_specs=[hbm, hbm, pl.BlockSpec...  72.7 us

profile of v3, /device:TPU:1, one launch (start us, length us, event | category | flops | bytes accessed | tf_op | source)
XLA Modules:
  0.0 74.8 jit_solution(16843183201736980986)
XLA Ops:
  1.3 72.7 %shard_map.121 = (bf16[128,1024]{1,0:T(8,128)(2,1)S(1)}, bf16[8,1024]{1,0:T(8,128)(2,1)S(1)}, f32[64,1024]{1,0:T(8,128)S(1)}) custom-call(bf16[128,1024]{1,0:T(8,128)(2,1)} %bitcast.7, bf16[8,1024]{1,0:T(8,128)(2,1)} %bitcast.9, s32[1]{0:T(128)S(6)} %copy.13.lengths, f32[1,1024]{1,0:T(1,128)} %bitcast.11, bf16[64,1024]{1,0:T(8,128)(2,1)} %w_query.1, ...), custom_call_target="tpu_custom_call" | custom-call | tf_op jit(solution)/shard_map/pallas_call | solution.py:489
  74.0 0.8 %shard_map.122 = (bf16[128,1024]{1,0:T(8,128)(2,1)}, bf16[8,1024]{1,0:T(8,128)(2,1)}, f32[64,1024]{1,0:T(8,128)}) custom-call(bf16[128,1024]{1,0:T(8,128)(2,1)S(1)} %get-tuple-element.9.fo_v, bf16[8,1024]{1,0:T(8,128)(2,1)S(1)} %get-tuple-element.10.mo_v, f32[64,1024]{1,0:T(8,128)S(1)} %get-tuple-element.11.vg_v), custom_call_target="tpu_custom_call" | custom-call | tf_op jit(solution)/shard_map/pallas_call | solution.py:503

commit v4 on v3

--- a/solution.py
+++ b/solution.py
@@ -214,9 +214,6 @@
     bank1 = E[1, 144:160, :].astype(F32)[:8]
     X[1, 144:160, :] = jnp.concatenate([bank0, bank1], axis=0).astype(BF16)
 
-    stage3(OUT)
-    stage2(QUERY)
-    stage3(KEY)
 
     tail_over.wait_recv()
     bank_over.wait_recv()
@@ -229,6 +226,9 @@
             XT[0, k, i] = block[64 * i:64 * i + 32]
             XT[1, i, k] = block[64 * i + 32:64 * i + 64]
 
+    stage2(QUERY)
+    stage3(OUT)
+    stage3(KEY)
     stage4(OUT)
     pass_word(0)
     out_over = remote(W.at[OUT, pl.ds(2 * other, 2)], WO2.at[core], device(flip=True))
@@ -260,32 +260,6 @@
     stage4(KEY)
     project_keys(KEY, K)
     pass_word(2)
-    stage1(VALUE)
-    stage4(QUERY)
-    query_rows = E[:, 0:144, :].reshape(288, 1024)
-    for n in range(2):
-        w = W[QUERY, :, :, :, :, 256 * n:256 * n + 256].reshape(1024, 256)
-        out = mm(query_rows, w).astype(BF16)
-        for g in range(2):
-            for p in range(2):
-                Q[g, 2 * n + p] = out[144 * g:144 * g + 144, 128 * p:128 * p + 128]
-
-    def attend(i, carry):
-        g = lax.div(i, 4)
-        p = lax.rem(i, 4)
-        scores = lax.dot_general(
-            K[g, p], Q[g, p], (((1,), (1,)), ((), ())), preferred_element_type=F32)
-        for h in range(2):
-            s = scores[160 * h:160 * h + 160] * 0.125 + bias[g]
-            e = jnp.exp(s - jnp.max(s, axis=0, keepdims=True))
-            total = jnp.sum(e, axis=0, keepdims=True)
-            PT[g, p, 160 * h:160 * h + 160, :] = (e / total).astype(BF16)
-        return carry
-
-    lax.fori_loop(0, 8, attend, 0)
-
-    pass_word(3)
-    stage2(VALUE)
     grads_over.wait_recv()
     out_here.wait()
     out_over.wait_recv()
@@ -298,6 +272,32 @@
         ga = (ga * live_of(g, (144, 1))).astype(BF16)
         for p in range(4):
             GA[g, p] = ga[:, 128 * p:128 * p + 128]
+    stage4(QUERY)
+    query_rows = E[:, 0:144, :].reshape(288, 1024)
+    for n in range(2):
+        w = W[QUERY, :, :, :, :, 256 * n:256 * n + 256].reshape(1024, 256)
+        out = mm(query_rows, w).astype(BF16)
+        for g in range(2):
+            for p in range(2):
+                Q[g, 2 * n + p] = out[144 * g:144 * g + 144, 128 * p:128 * p + 128]
+
+    stage1(VALUE)
+
+    def attend(i, carry):
+        g = lax.div(i, 4)
+        p = lax.rem(i, 4)
+        scores = lax.dot_general(
+            K[g, p], Q[g, p], (((1,), (1,)), ((), ())), preferred_element_type=F32)
+        for h in range(2):
+            s = scores[160 * h:160 * h + 160] * 0.125 + bias[g]
+            e = jnp.exp(s - jnp.max(s, axis=0, keepdims=True))
+            total = jnp.sum(e, axis=0, keepdims=True)
+            PT[g, p, 160 * h:160 * h + 160, :] = (e / total).astype(BF16)
+        return carry
+
+    lax.fori_loop(0, 8, attend, 0)
+
+    pass_word(3)
     pass_word(4)
     for g in range(2):
         for p in range(4):
@@ -338,7 +338,7 @@
         SA[d, h] = (G[g_part(d, s, h)].astype(F32) + RA1[d, h].astype(F32)).astype(BF16)
         a2a[d, s] = remote(SA.at[d, h], RA2A.at[d, h], a_to(d, s))
 
-    stage3(VALUE)
+    stage2(VALUE)
 
     for d in range(2):
         for s in (1, -1):
@@ -363,8 +363,7 @@
             to = ((quad * 4 + to_place) * 2 + core, to_y * 4 + to_x)
             z1.append(remote(RS.at[d, wrap(along, o), lax.rem(to_place, 2)], RZ.at[o, k], to))
 
-    stage4(VALUE)
-    project_keys(VALUE, V)
+    stage3(VALUE)
 
     for copy in z1:
         copy.wait_recv()
@@ -376,6 +375,9 @@
                 part = part + RZ[o, k].astype(F32)
     ZQ[quad] = part.astype(BF16)
     z2 = {s: remote(ZQ.at[quad], ZQ.at[quad], device(dz=4 * s)) for s in (1, -1)}
+
+    stage4(VALUE)
+    project_keys(VALUE, V)
 
     def attended(i, carry):
         g = lax.div(i, 4)

time: 75 us -> 77.4 us (1.032)
  Pallas kernels: 73.5 us -> 76 us
    pallas_call x1, Pallas kernels: 72.7 us -> 75.2 us  [on_device(): pl.pallas_call(kernel, out_shape=shapes, in_specs=[hbm, hbm, pl.BlockSpec...]
where the time goes in v4:
time: 77.4 us; the launch traced here: 77.3 us
  Pallas kernels  76 us (98%)
  between operations  1.29 us (2%)
    pallas_call x1, Pallas kernels, on_device(): pl.pallas_call(kernel, out_shape=shapes, in_specs=[hbm, hbm, pl.BlockSpec...  75.2 us

profile of v4, /device:TPU:1, one launch (start us, length us, event | category | flops | bytes accessed | tf_op | source)
XLA Modules:
  0.0 77.3 jit_solution(12557105447554568820)
XLA Ops:
  1.3 75.2 %shard_map.121 = (bf16[128,1024]{1,0:T(8,128)(2,1)S(1)}, bf16[8,1024]{1,0:T(8,128)(2,1)S(1)}, f32[64,1024]{1,0:T(8,128)S(1)}) custom-call(bf16[128,1024]{1,0:T(8,128)(2,1)} %bitcast.7, bf16[8,1024]{1,0:T(8,128)(2,1)} %bitcast.9, s32[1]{0:T(128)S(6)} %copy.13.lengths, f32[1,1024]{1,0:T(1,128)} %bitcast.11, bf16[64,1024]{1,0:T(8,128)(2,1)} %w_query.1, ...), custom_call_target="tpu_custom_call" | custom-call | tf_op jit(solution)/shard_map/pallas_call | solution.py:491
  76.5 0.8 %shard_map.122 = (bf16[128,1024]{1,0:T(8,128)(2,1)}, bf16[8,1024]{1,0:T(8,128)(2,1)}, f32[64,1024]{1,0:T(8,128)}) custom-call(bf16[128,1024]{1,0:T(8,128)(2,1)S(1)} %get-tuple-element.9.fo_v, bf16[8,1024]{1,0:T(8,128)(2,1)S(1)} %get-tuple-element.10.mo_v, f32[64,1024]{1,0:T(8,128)S(1)} %get-tuple-element.11.vg_v), custom_call_target="tpu_custom_call" | custom-call | tf_op jit(solution)/shard_map/pallas_call | solution.py:505

commit v5 on v4

--- a/solution.py
+++ b/solution.py
@@ -298,6 +298,7 @@
     lax.fori_loop(0, 8, attend, 0)
 
     pass_word(3)
+    stage2(VALUE)
     pass_word(4)
     for g in range(2):
         for p in range(4):
@@ -338,7 +339,7 @@
         SA[d, h] = (G[g_part(d, s, h)].astype(F32) + RA1[d, h].astype(F32)).astype(BF16)
         a2a[d, s] = remote(SA.at[d, h], RA2A.at[d, h], a_to(d, s))
 
-    stage2(VALUE)
+    stage3(VALUE)
 
     for d in range(2):
         for s in (1, -1):
@@ -363,7 +364,8 @@
             to = ((quad * 4 + to_place) * 2 + core, to_y * 4 + to_x)
             z1.append(remote(RS.at[d, wrap(along, o), lax.rem(to_place, 2)], RZ.at[o, k], to))
 
-    stage3(VALUE)
+    stage4(VALUE)
+    project_keys(VALUE, V)
 
     for copy in z1:
         copy.wait_recv()
@@ -375,9 +377,6 @@
                 part = part + RZ[o, k].astype(F32)
     ZQ[quad] = part.astype(BF16)
     z2 = {s: remote(ZQ.at[quad], ZQ.at[quad], device(dz=4 * s)) for s in (1, -1)}
-
-    stage4(VALUE)
-    project_keys(VALUE, V)
 
     def attended(i, carry):
         g = lax.div(i, 4)

time: 77.4 us -> 77.4 us (level)
  no operation moved by 1% of the time
where the time goes in v5:
time: 77.4 us; the launch traced here: 77.3 us
  Pallas kernels  76 us (98%)
  between operations  1.29 us (2%)
    pallas_call x1, Pallas kernels, on_device(): pl.pallas_call(kernel, out_shape=shapes, in_specs=[hbm, hbm, pl.BlockSpec...  75.1 us

profile of v5, /device:TPU:1, one launch (start us, length us, event | category | flops | bytes accessed | tf_op | source)
XLA Modules:
  0.0 77.3 jit_solution(9342837312249609171)
XLA Ops:
  1.3 75.1 %shard_map.121 = (bf16[128,1024]{1,0:T(8,128)(2,1)S(1)}, bf16[8,1024]{1,0:T(8,128)(2,1)S(1)}, f32[64,1024]{1,0:T(8,128)S(1)}) custom-call(bf16[128,1024]{1,0:T(8,128)(2,1)} %bitcast.7, bf16[8,1024]{1,0:T(8,128)(2,1)} %bitcast.9, s32[1]{0:T(128)S(6)} %copy.13.lengths, f32[1,1024]{1,0:T(1,128)} %bitcast.11, bf16[64,1024]{1,0:T(8,128)(2,1)} %w_query.1, ...), custom_call_target="tpu_custom_call" | custom-call | tf_op jit(solution)/shard_map/pallas_call | solution.py:490
  76.4 0.8 %shard_map.122 = (bf16[128,1024]{1,0:T(8,128)(2,1)}, bf16[8,1024]{1,0:T(8,128)(2,1)}, f32[64,1024]{1,0:T(8,128)}) custom-call(bf16[128,1024]{1,0:T(8,128)(2,1)S(1)} %get-tuple-element.9.fo_v, bf16[8,1024]{1,0:T(8,128)(2,1)S(1)} %get-tuple-element.10.mo_v, f32[64,1024]{1,0:T(8,128)S(1)} %get-tuple-element.11.vg_v), custom_call_target="tpu_custom_call" | custom-call | tf_op jit(solution)/shard_map/pallas_call | solution.py:504
